TPU v7x, 512 devices: a whole 4x8x8 slice. The times are simulated.
512 devices in a mesh: row: 16 (over x, z_hi), col: 32 (over z_lo, y, core).
Axes of the slice: x: 4, y: 8, z: 8 (z_hi: 4, z_lo: 2; z = z_hi * 2 + z_lo), core: 2. Of those that a mesh axis runs over, the one named last changes fastest.
Arguments:
- bin_features: bfloat16 [4096, 512], P('row'), may hold values from -6 to 6
- w_left: bfloat16 [512, 32], replicated, may hold values from -0.25 to 0.25
- w_right: bfloat16 [512, 32], replicated, may hold values from -0.25 to 0.25
- depth_kernel: float32 [9, 32], replicated, may hold values from -2 to 2
- w_point: bfloat16 [32, 32], replicated, may hold values from -1 to 1
- w_head: bfloat16 [32, 24], replicated, may hold values from -1 to 1
- cotangent: bfloat16 [24, 4096, 4096], P(None, 'row', 'col'), may hold values from -6 to 6
Outputs:
- grad_features: bfloat16 [4096, 512], P('row')
- grad_w_left: float32 [512, 32], replicated
- grad_w_right: float32 [512, 32], replicated
- grad_kernel: float32 [9, 32], replicated
- grad_point: float32 [32, 32], replicated
- grad_head: float32 [32, 24], replicated
All inputs are finite; a program needn't handle non-finite values.
Results may differ from a plain program's by a relative error of at most 0.019.
Values may be sent and summed in bfloat16 or wider, within the bound.
No kernel may reach another device: no remote copies, remote signals or barrier semaphores. Data moves between devices by JAX's collectives and lax.ppermute only.
A program may use at most 64 MiB of HBM per device.

v0:
```python
import math
import jax
import jax.numpy as jnp
from jax import lax
from jax.sharding import PartitionSpec as P

DILATION_STEP = 4


def from_root(block, axis, source):
    block = jnp.where(lax.axis_index(axis) == source, block, jnp.zeros_like(block))
    return lax.psum(block, axis)


def extended(x, sides, width):
    for axis, dim in sides:
        count, length = (lax.axis_size(axis), x.shape[dim])
        up = [(i, (i + 1) % count) for i in range(count - 1)]
        down = [(j, i) for i, j in up]
        last = lax.slice_in_dim(x, length - width, length, axis=dim)
        first = lax.slice_in_dim(x, 0, width, axis=dim)
        before = lax.ppermute(last, axis, up)
        after = lax.ppermute(first, axis, down)
        x = jnp.concatenate([before, x, after], axis=dim)
    return x


def silu_slope(values):
    logistic = jax.nn.sigmoid(values)
    return logistic * (1.0 + values * (1.0 - logistic))


def depthwise(kernel_taps, padded, output_rows, output_columns):
    result = jnp.zeros((padded.shape[0], output_rows, output_columns), jnp.float32)
    for kernel_tap_row in range(3):
        for kernel_tap_column in range(3):
            result = result + kernel_taps[3 * kernel_tap_row + kernel_tap_column][
                :, None, None
            ] * padded[
                :,
                DILATION_STEP * kernel_tap_row : DILATION_STEP * kernel_tap_row + output_rows,
                DILATION_STEP * kernel_tap_column : DILATION_STEP * kernel_tap_column
                + output_columns,
            ].astype(
                jnp.float32
            )
    return result


def body(bin_features, w_left, w_right, depth_kernel, w_point, w_head, cotangent):
    rows_per_tile = bin_features.shape[0]
    columns_per_tile = cotangent.shape[2]
    chans = w_left.shape[1]
    row_count = lax.axis_size("row")
    col_count = lax.axis_size("col")
    panel_ratio = col_count // row_count
    contact_map_bins = rows_per_tile * row_count
    grad_scale = 1.0 / math.sqrt(contact_map_bins)
    row_index = lax.axis_index("row")
    col_index = lax.axis_index("col")
    left_panel = jnp.dot(bin_features, w_left, preferred_element_type=jnp.float32).astype(
        jnp.bfloat16
    )
    offset = col_index % panel_ratio * columns_per_tile
    own_rows = lax.dynamic_slice_in_dim(bin_features, offset, columns_per_tile, 0)
    right_own = jnp.dot(own_rows, w_right, preferred_element_type=jnp.float32).astype(jnp.bfloat16)
    right_panel = from_root(right_own, "row", col_index // panel_ratio)
    pair_matrix = (
        left_panel.astype(jnp.float32).T[:, :, None] + right_panel.astype(jnp.float32).T[:, None, :]
    ).astype(jnp.bfloat16)
    extended_pair = extended(pair_matrix, (("row", 1), ("col", 2)), DILATION_STEP)
    convolved_map = depthwise(depth_kernel, extended_pair, rows_per_tile, columns_per_tile)
    trunk_gradient = (
        grad_scale
        * jnp.einsum("ch,hij->cij", w_head, cotangent, preferred_element_type=jnp.float32)
    ).astype(jnp.bfloat16)
    grad_hidden = jnp.einsum(
        "co,oij->cij", w_point, trunk_gradient, preferred_element_type=jnp.float32
    )
    convolved_gradient = (grad_hidden * silu_slope(convolved_map)).astype(jnp.bfloat16)
    extended_gradient = extended(convolved_gradient, (("row", 1), ("col", 2)), DILATION_STEP)
    hidden_state = jax.nn.silu(convolved_map).astype(jnp.bfloat16)
    mixed_out = jnp.einsum("co,cij->oij", w_point, hidden_state, preferred_element_type=jnp.float32)
    centre_offset = extended_pair[
        :,
        DILATION_STEP : DILATION_STEP + rows_per_tile,
        DILATION_STEP : DILATION_STEP + columns_per_tile,
    ]
    trunk_matrix = (centre_offset.astype(jnp.float32) + mixed_out).astype(jnp.bfloat16)
    conv_f32 = convolved_gradient.astype(jnp.float32)
    backward_pass = jnp.zeros((chans, rows_per_tile, columns_per_tile), jnp.float32)
    kern_terms = []
    for kernel_tap_row in range(3):
        for kernel_tap_column in range(3):
            backward_pass = backward_pass + depth_kernel[3 * kernel_tap_row + kernel_tap_column][
                :, None, None
            ] * extended_gradient[
                :,
                DILATION_STEP * (2 - kernel_tap_row) : DILATION_STEP * (2 - kernel_tap_row)
                + rows_per_tile,
                DILATION_STEP * (2 - kernel_tap_column) : DILATION_STEP * (2 - kernel_tap_column)
                + columns_per_tile,
            ].astype(
                jnp.float32
            )
            shifted_window = extended_pair[
                :,
                DILATION_STEP * kernel_tap_row : DILATION_STEP * kernel_tap_row + rows_per_tile,
                DILATION_STEP * kernel_tap_column : DILATION_STEP * kernel_tap_column
                + columns_per_tile,
            ].astype(jnp.float32)
            kern_terms.append(jnp.sum(conv_f32 * shifted_window, axis=(1, 2)))
    kernel_part = jnp.stack(kern_terms)
    pair_gradient = trunk_gradient.astype(jnp.float32) + backward_pass
    left_part = jnp.sum(pair_gradient, axis=2).T
    right_part = jnp.sum(pair_gradient, axis=1).T
    point_part = jnp.einsum(
        "fsk,gsk->fg", hidden_state, trunk_gradient, preferred_element_type=jnp.float32
    )
    head_part = jnp.einsum(
        "ydq,gdq->yg", trunk_matrix, cotangent, preferred_element_type=jnp.float32
    )
    grad_left = lax.psum(left_part, "col").astype(jnp.bfloat16)
    column_total = lax.psum(right_part, "row").astype(jnp.bfloat16)
    all_panels = lax.all_gather(column_total, "col", axis=0, tiled=True)
    grad_right = lax.dynamic_slice_in_dim(all_panels, row_index * rows_per_tile, rows_per_tile, 0)
    grad_features = (
        jnp.dot(grad_left, w_left.T, preferred_element_type=jnp.float32)
        + jnp.dot(grad_right, w_right.T, preferred_element_type=jnp.float32)
    ).astype(jnp.bfloat16)
    contract = (((0,), (0,)), ((), ()))
    wleft_part = lax.dot_general(
        bin_features, grad_left, contract, preferred_element_type=jnp.float32
    )
    wright_part = lax.dot_general(
        bin_features, grad_right, contract, preferred_element_type=jnp.float32
    )
    kernel_sum, point_sum, head_sum = lax.psum((kernel_part, point_part, head_part), ("row", "col"))
    wleft_sum, wright_sum = lax.psum((wleft_part, wright_part), "row")
    return (
        grad_features,
        grad_scale * wleft_sum,
        grad_scale * wright_sum,
        grad_scale * kernel_sum,
        grad_scale * point_sum,
        grad_scale * head_sum,
    )


def solution(mesh):
    placed = (P("row", None), P(), P(), P(), P(), P(), P(None, "row", "col"))
    return jax.shard_map(
        body,
        mesh=mesh,
        in_specs=placed,
        out_specs=(P("row", None), P(), P(), P(), P(), P()),
        check_vma=False,
    )
```

profile of v0, /device:TPU:8, one launch (start us, length us, event | category | flops | bytes accessed | tf_op | source)
XLA Modules:
  0.0 674.3 jit_solution(18254187634809960480)
XLA Ops:
  8.4 50.8 %psum.56 = bf16[32,128]{1,0:T(8,128)(2,1)S(1)} all-reduce(bf16[32,128]{1,0:T(8,128)(2,1)S(1)} %fusion.34), channel_id=1, replica_groups=mesh['row'=16,'col'=32] {'row'}, use_global_device_ids=true, to_apply=%region_0.1 | all-reduce | flops 4096 | bytes 16384 | tf_op jit(solution)/shard_map/psum | solution.py:12
  64.8 3.5 multiply_convert_fusion.1
  73.5 3.6 copy.20
  77.1 3.6 copy.22
  85.3 3.3 collective-permute-done.2
  88.6 3.0 copy.21
  91.6 3.0 copy.23
  94.7 7.2 %maximum_maximum_fusion = (bf16[32,264,132]{2,0,1:T(8,128)(2,1)S(1)}, bf16[32,264,132]{2,0,1:T(8,128)(2,1)S(1)}) fusion(bf16[32,4,128]{2,0,1:T(8,128)(2,1)S(1)} %collective-permute-done.1, bf16[32,256,128]{2,0,1:T(8,128)(2,1)} %copy-done.1, bf16[32,4,128]{2,0,1:T(8,128)(2,1)S(1)} %collective-permute-done, bf16[32,264,4]{2,0,1:T(8,128)(2,1)} %copy.21, ...), kind=kLoop, calls=%fused_computation.20 | loop fusion | flops 17842176 | bytes 6758400 | tf_op jit(solution)/shard_map/concatenate | solution.py:24
  101.9 10.2 %multiply_convert_fusion = (bf16[32,256,128]{2,0,1:T(8,128)(2,1)}, f32[32,256,128]{2,0,1:T(8,128)}) fusion(bf16[32,264,132]{2,0,1:T(8,128)(2,1)S(1)} %get-tuple-element.34, f32[32]{0:T(128)S(1)} %get-tuple-element.48, bf16[32,4,128]{2,0,1:T(8,128)(2,1)S(1)} %collective-permute-done.1, bf16[32,256,128]{2,0,1:T(8,128)(2,1)S(1)} %copy-done.2, ...), kind=kLoop, calls=%fused_computation.50 | loop fusion | flops 36700160 | bytes 21087360 | tf_op jit(solution)/shard_map/convert_element_type | solution.py:82
  112.1 3.4 fusion.30
  115.6 3.0 convolution_bitcast_fusion.2
  119.0 13.2 %fusion.23 = (f32[32]{0:T(128)S(1)}, f32[32]{0:T(128)S(1)}, f32[32]{0:T(128)S(1)}, f32[32]{0:T(128)S(1)}, f32[32]{0:T(128)S(1)}, /*index=5*/f32[32]{0:T(128)S(1)...) fusion(bf16[32,264,132]{2,0,1:T(8,128)(2,1)} %copy-done.5, ...), kind=kOutput, calls=%fused_computation.47 | convolution fusion | flops 110100192 | bytes 23186560 | tf_op jit(solution)/shard_map/co,oij->cij/dot_general | solution.py:77
  132.3 96.0 %all-reduce = (f32[9,32]{1,0:T(8,128)S(1)}, f32[32,32]{1,0:T(8,128)S(1)}, f32[32,24]{0,1:T(8,128)S(1)}) all-reduce(f32[9,32]{1,0:T(8,128)S(1)} %stack.39, f32[32,32]{1,0:T(8,128)S(1)} %convolution_bitcast_fusion.2, f32[32,24]{0,1:T(8,128)S(1)} %fusion.30), channel_id=1, replica_groups=mesh['row'=16,'col'=32] {'row','col'}, use_global_device_ids=true, to_apply=%region_16.17 | all-reduce | flops 2080 | bytes 16640 | tf_op jit(solution)/shard_map/psum | solution.py:138
  234.6 5.1 collective-permute-done.5
  244.5 3.6 copy.24
  248.1 3.6 copy.26
  253.7 3.6 collective-permute-start.6
  262.6 3.0 copy.27
  265.6 7.2 %pad_maximum_fusion.1 = (bf16[32,264,132]{2,0,1:T(8,128)(2,1)S(1)}, bf16[32,264,132]{2,0,1:T(8,128)(2,1)S(1)}) fusion(bf16[32,264,4]{2,0,1:T(8,128)(2,1)} %copy.25, bf16[32,4,128]{2,0,1:T(8,128)(2,1)S(1)} %collective-permute-done.5, bf16[32,256,128]{2,0,1:T(8,128)(2,1)} %get-tuple-element.50, bf16[32,4,128]{2,0,1:T(8,128)(2,1)S(1)} %collective-permute-done.4, ...), kind=kLoop, calls=%fused_computation.22 | loop fusion | flops 17842176 | bytes 6758400 | tf_op jit(solution)/shard_map/concatenate | solution.py:24
  272.9 7.2 %fusion.48 = (f32[32,128]{1,0:T(8,128)S(1)}, f32[32,256]{0,1:T(8,128)S(1)}) fusion(bf16[32,264,132]{2,0,1:T(8,128)(2,1)S(1)} %get-tuple-element.30, f32[32]{0:T(128)S(1)} %get-tuple-element.48, bf16[32,256,128]{2,0,1:T(8,128)(2,1)S(1)} %copy-done.6, bf16[32,4,128]{2,0,1:T(8,128)(2,1)S(1)} %collective-permute-done.4, f32[32]{0:T(128)S(1)} %get-tuple-element.49, ...), kind=kLoop, calls=%fused_computation.100 | loop fusion | flops 33542144 | bytes 16893056 | tf_op jit(solution)/shard_map/reduce_sum | solution.py:116
  280.2 102.3 %psum.57 = bf16[256,32]{1,0:T(8,128)(2,1)S(1)} all-reduce(f32[256,32]{1,0:T(8,128)S(1)} %bitcast.73), channel_id=1, replica_groups=mesh['row'=16,'col'=32] {'col'}, use_global_device_ids=true, to_apply=%region_2.3 | all-reduce | flops 8192 | bytes 49152 | tf_op jit(solution)/shard_map/psum | solution.py:123
  383.5 80.7 %psum.58 = bf16[128,32]{0,1:T(8,128)(2,1)S(1)} all-reduce(f32[128,32]{0,1:T(8,128)S(1)} %bitcast.74), channel_id=1, replica_groups=mesh['row'=16,'col'=32] {'row'}, use_global_device_ids=true, to_apply=%region_4.5 | all-reduce | flops 4096 | bytes 24576 | tf_op jit(solution)/shard_map/psum | solution.py:124
  464.2 35.4 %all_gather.3 = bf16[4096,32]{0,1:T(8,128)(2,1)S(1)} all-gather(bf16[128,32]{0,1:T(8,128)(2,1)S(1)} %psum.58), channel_id=1, replica_groups=mesh['row'=16,'col'=32] {'col'}, dimensions={0}, use_global_device_ids=true | all-gather | bytes 270336 | tf_op jit(solution)/shard_map/all_gather | solution.py:125
  501.3 164.6 %all-reduce.4.cloned.1.call-done = (f32[512,32]{0,1:T(8,128)}, f32[512,32]{0,1:T(8,128)}) async-done(((f32[512,32]{0,1:T(8,128)}, f32[512,32]{0,1:T(8,128)}), (f32[512,32]{0,1:T(8,128)}, f32[512,32]{0,1:T(8,128)})) %all-reduce.4.cloned.1.call-update) | async-done | bytes 131088 | tf_op jit(solution)/shard_map/psum | solution.py:139
  (65 shorter events, 39.5 us)
Async XLA Ops:
  7.2 57.7 %copy-start = (bf16[24,256,128]{2,1,0:T(8,128)(2,1)S(1)}, bf16[24,256,128]{2,1,0:T(8,128)(2,1)}, u32[]{:S(2)}) copy-start(bf16[24,256,128]{2,1,0:T(8,128)(2,1)} %param.13) | copy-start | bytes 4718596
  7.2 658.8 %all-reduce.4.cloned.1.call-start = ((), (), s32[]{:S(2)}) async-start(), calls=%async_computation | async-start | bytes 262144 | tf_op jit(solution)/shard_map/psum | solution.py:139
  62.2 8.0 %copy-start.1 = (bf16[32,256,128]{2,0,1:T(8,128)(2,1)}, bf16[32,256,128]{2,0,1:T(8,128)(2,1)S(1)}, u32[]{:S(2)}) copy-start(bf16[32,256,128]{2,0,1:T(8,128)(2,1)S(1)} %add_convert_fusion) | copy-start | bytes 6291460
  62.2 6.1 collective-permute-start
  63.5 6.7 collective-permute-start.1
  73.5 11.8 %copy-start.12 = (f32[9,32]{1,0:T(8,128)S(1)}, f32[9,32]{1,0:T(8,128)}, u32[]{:S(2)}) copy-start(f32[9,32]{1,0:T(8,128)} %param.10) | copy-start | bytes 3460
  80.8 10.9 %collective-permute-start.3 = (bf16[32,264,4]{1,0,2:T(8,128)(2,1)S(1)}, bf16[32,264,4]{1,0,2:T(8,128)(2,1)S(1)}, u32[]{:S(2)}, u32[]{:S(2)}) collective-permute-start(bf16[32,264,4]{1,0,2:T(8,128)(2,1)S(1)} %copy.22), channel_id=1, source_target_pairs={{1,0},{2,1},{3,2},{4,3},{5,4},{6,5},{7,6},{8,7},{9,8},{10,9},{11,1... | collective-permute-start | bytes 202760 | tf_op jit(solution)/shard_map/ppermute | solution.py:23
  82.7 5.9 collective-permute-start.2
  94.7 7.2 %copy-start.2 = (bf16[32,256,128]{2,0,1:T(8,128)(2,1)S(1)}, bf16[32,256,128]{2,0,1:T(8,128)(2,1)}, u32[]{:S(2)}) copy-start(bf16[32,256,128]{2,0,1:T(8,128)(2,1)} %copy-done.1) | copy-start | bytes 6291460
  101.9 10.2 %copy-start.4 = (bf16[32,264,132]{2,0,1:T(8,128)(2,1)}, bf16[32,264,132]{2,0,1:T(8,128)(2,1)S(1)}, u32[]{:S(2)}) copy-start(bf16[32,264,132]{2,0,1:T(8,128)(2,1)S(1)} %get-tuple-element.33) | copy-start | bytes 6690820
  101.9 10.2 %copy-start.5 = (bf16[32,264,132]{2,0,1:T(8,128)(2,1)}, bf16[32,264,132]{2,0,1:T(8,128)(2,1)S(1)}, u32[]{:S(2)}) copy-start(bf16[32,264,132]{2,0,1:T(8,128)(2,1)S(1)} %get-tuple-element.34) | copy-start | bytes 6690820
  101.9 10.2 %copy-start.13 = (bf16[32,32]{1,0:T(8,128)(2,1)S(1)}, bf16[32,32]{1,0:T(8,128)(2,1)}, u32[]{:S(2)}) copy-start(bf16[32,32]{1,0:T(8,128)(2,1)} %param.11) | copy-start | bytes 6148
  115.5 3.1 copy-start.3
  115.5 3.5 copy-start.7
  229.7 4.9 collective-permute-start.4
  232.5 7.2 %collective-permute-start.5 = (bf16[32,4,128]{2,0,1:T(8,128)(2,1)S(1)}, bf16[32,4,128]{2,0,1:T(8,128)(2,1)S(1)}, u32[]{:S(2)}, u32[]{:S(2)}) collective-permute-start(bf16[32,4,128]{2,0,1:T(8,128)(2,1)S(1)} %get-tuple-element.38), channel_id=1, source_target_pairs={{32,0},{64,32},{96,64},{128,96},{160,128},{192,160},{224,192},{256... | collective-permute-start | bytes 98312 | tf_op jit(solution)/shard_map/ppermute | solution.py:23
  251.8 10.8 %collective-permute-start.7 = (bf16[32,264,4]{1,0,2:T(8,128)(2,1)S(1)}, bf16[32,264,4]{1,0,2:T(8,128)(2,1)S(1)}, u32[]{:S(2)}, u32[]{:S(2)}) collective-permute-start(bf16[32,264,4]{1,0,2:T(8,128)(2,1)S(1)} %copy.26), channel_id=1, source_target_pairs={{0,1},{1,2},{2,3},{3,4},{4,5},{5,6},{6,7},{7,8},{8,9},{9,10},{10,1... | collective-permute-start | bytes 202760 | tf_op jit(solution)/shard_map/ppermute | solution.py:22
  253.7 5.8 collective-permute-start.6
  265.6 7.3 %copy-start.6 = (bf16[32,256,128]{2,0,1:T(8,128)(2,1)S(1)}, bf16[32,256,128]{2,0,1:T(8,128)(2,1)}, u32[]{:S(2)}) copy-start(bf16[32,256,128]{2,0,1:T(8,128)(2,1)} %get-tuple-element.50) | copy-start | bytes 6291460
  265.6 7.3 %copy-start.8 = (bf16[32,256,128]{2,0,1:T(8,128)(2,1)S(1)}, bf16[32,256,128]{2,0,1:T(8,128)(2,1)}, u32[]{:S(2)}) copy-start(bf16[32,256,128]{2,0,1:T(8,128)(2,1)} %multiply_convert_fusion.1) | copy-start | bytes 6291460
  272.9 109.6 %copy-start.9 = (bf16[256,512]{1,0:T(8,128)(2,1)S(1)}, bf16[256,512]{1,0:T(8,128)(2,1)}, u32[]{:S(2)}) copy-start(bf16[256,512]{1,0:T(8,128)(2,1)} %param.7) | copy-start | bytes 786436
  272.9 110.4 %copy-start.10 = (bf16[512,32]{0,1:T(8,128)(2,1)S(1)}, bf16[512,32]{0,1:T(8,128)(2,1)}, u32[]{:S(2)}) copy-start(bf16[512,32]{0,1:T(8,128)(2,1)} %param.8) | copy-start | bytes 98308
  272.9 227.5 %copy-start.11 = (bf16[512,32]{0,1:T(8,128)(2,1)S(1)}, bf16[512,32]{0,1:T(8,128)(2,1)}, u32[]{:S(2)}) copy-start(bf16[512,32]{0,1:T(8,128)(2,1)} %param.9) | copy-start | bytes 98308
Sparse Core Ops, SparseCore 0:
  500.5 165.3 all-reduce.3
where the time goes:
time: 675 us; the launch traced here: 674 us
  blocking collectives  365 us (54%)
  waiting for transfers between devices  176 us (26%)
  other arithmetic  39 us (6%)
  local copies, waits for them, and re-layouts  34 us (5%)
  matrix products  28.2 us (4%)
  starting transfers between devices  17 us (3%)
  between operations  14.4 us (2%)
    psum x1, waiting for transfers between devices, body(): wleft_sum, wright_sum = lax.psum((wleft_part, wright_part), 'row')  165 us
    psum x1, blocking collectives, body(): grad_left = lax.psum(left_part, 'col').astype(jnp.bfloat16)  102 us
    psum x1, blocking collectives, body(): lax.psum((kernel_part, point_part, head_part), ('row', 'col'))  96 us
    psum x1, blocking collectives, body(): column_total = lax.psum(right_part, 'row').astype(jnp.bfloat16)  80.7 us
    psum x1, blocking collectives, from_root(): return lax.psum(block, axis)  50.8 us
    all_gather x1, blocking collectives, body(): all_panels = lax.all_gather(column_total, 'col', axis=0, tiled=True)  35.4 us
    concatenate x4, other arithmetic, extended(): x = jnp.concatenate([before, x, after], axis=dim)  16.6 us
  transfers between devices with their start and end apart: 9, of which 5 were waited for; matrix products, arithmetic and copies ran while one was open for 2% of the time, Pallas kernels for 0%

commit v1 on v0

--- a/solution.py
+++ b/solution.py
@@ -122,7 +122,9 @@
     )
     grad_left = lax.psum(left_part, "col").astype(jnp.bfloat16)
     column_total = lax.psum(right_part, "row").astype(jnp.bfloat16)
-    all_panels = lax.all_gather(column_total, "col", axis=0, tiled=True)
+    all_panels = jnp.concatenate(
+        lax.all_to_all(jnp.stack([column_total] * lax.axis_size("col")), "col", 0, 0), axis=0
+    )
     grad_right = lax.dynamic_slice_in_dim(all_panels, row_index * rows_per_tile, rows_per_tile, 0)
     grad_features = (
         jnp.dot(grad_left, w_left.T, preferred_element_type=jnp.float32)

time: 675 us -> 647 us (0.959)
  blocking collectives: 365 us -> 333 us
  starting transfers between devices: 17 us -> 27.1 us
    all_gather x1 -> x0, blocking collectives: 35.4 us -> none  [body(): all_panels = lax.all_gather(column_total, 'col', axis=0, tiled=True)]
    all_to_all x0 -> x1, starting transfers between devices: none -> 8.63 us  [body(): lax.all_to_all(jnp.stack([column_total] * lax.axis_size('col')), 'col', 0...]
  transfers between devices with their start and end apart: 9 -> 10, of which waited for: 5 -> 4; matrix products, arithmetic and copies ran while one was open for 2% -> 2% of each run, Pallas kernels for 0% -> 0%
where the time goes in v1:
time: 647 us; the launch traced here: 646 us
  blocking collectives  333 us (51%)
  waiting for transfers between devices  170 us (26%)
  other arithmetic  39 us (6%)
  local copies, waits for them, and re-layouts  35.3 us (5%)
  matrix products  27.2 us (4%)
  starting transfers between devices  27.1 us (4%)
  between operations  14.4 us (2%)
    psum x1, waiting for transfers between devices, body(): wleft_sum, wright_sum = lax.psum((wleft_part, wright_part), 'row')  163 us
    psum x1, blocking collectives, body(): grad_left = lax.psum(left_part, 'col').astype(jnp.bfloat16)  104 us
    psum x1, blocking collectives, body(): lax.psum((kernel_part, point_part, head_part), ('row', 'col'))  98.4 us
    psum x1, blocking collectives, body(): column_total = lax.psum(right_part, 'row').astype(jnp.bfloat16)  79.5 us
    psum x1, blocking collectives, from_root(): return lax.psum(block, axis)  50.8 us
    concatenate x4, other arithmetic, extended(): x = jnp.concatenate([before, x, after], axis=dim)  16.6 us
  transfers between devices with their start and end apart: 10, of which 4 were waited for; matrix products, arithmetic and copies ran while one was open for 2% of the time, Pallas kernels for 0%

profile of v1, /device:TPU:8, one launch (start us, length us, event | category | flops | bytes accessed | tf_op | source)
XLA Modules:
  0.0 645.9 jit_solution(14249898495257398312)
XLA Ops:
  8.4 50.8 %psum.56 = bf16[32,128]{1,0:T(8,128)(2,1)S(1)} all-reduce(bf16[32,128]{1,0:T(8,128)(2,1)S(1)} %fusion.34), channel_id=1, replica_groups=mesh['row'=16,'col'=32] {'row'}, use_global_device_ids=true, to_apply=%region_0.1 | all-reduce | flops 4096 | bytes 16384 | tf_op jit(solution)/shard_map/psum | solution.py:12
  64.8 3.5 multiply_convert_fusion.1
  73.4 3.6 copy.34
  77.1 3.6 copy.36
  85.3 3.3 collective-permute-done.2
  88.6 3.0 copy.35
  91.6 3.0 copy.37
  94.6 7.2 %maximum_maximum_fusion = (bf16[32,264,132]{2,0,1:T(8,128)(2,1)S(1)}, bf16[32,264,132]{2,0,1:T(8,128)(2,1)S(1)}) fusion(bf16[32,4,128]{2,0,1:T(8,128)(2,1)S(1)} %collective-permute-done.1, bf16[32,256,128]{2,0,1:T(8,128)(2,1)} %copy-done.1, bf16[32,4,128]{2,0,1:T(8,128)(2,1)S(1)} %collective-permute-done, bf16[32,264,4]{2,0,1:T(8,128)(2,1)} %copy.35, ...), kind=kLoop, calls=%fused_computation.20 | loop fusion | flops 17842176 | bytes 6758400 | tf_op jit(solution)/shard_map/concatenate | solution.py:24
  101.9 10.2 %multiply_convert_fusion = (bf16[32,256,128]{2,0,1:T(8,128)(2,1)}, f32[32,256,128]{2,0,1:T(8,128)}) fusion(bf16[32,264,132]{2,0,1:T(8,128)(2,1)S(1)} %get-tuple-element.34, f32[32]{0:T(128)S(1)} %get-tuple-element.48, bf16[32,4,128]{2,0,1:T(8,128)(2,1)S(1)} %collective-permute-done.1, bf16[32,256,128]{2,0,1:T(8,128)(2,1)S(1)} %copy-done.2, ...), kind=kLoop, calls=%fused_computation.50 | loop fusion | flops 36700160 | bytes 21087360 | tf_op jit(solution)/shard_map/convert_element_type | solution.py:82
  112.1 3.4 fusion.30
  115.5 3.0 convolution_bitcast_fusion.2
  119.0 12.2 %fusion.23 = (f32[32]{0:T(128)S(1)}, f32[32]{0:T(128)S(1)}, f32[32]{0:T(128)S(1)}, f32[32]{0:T(128)S(1)}, f32[32]{0:T(128)S(1)}, /*index=5*/f32[32]{0:T(128)S(1)...) fusion(bf16[32,264,132]{2,0,1:T(8,128)(2,1)} %copy-done.5, ...), kind=kOutput, calls=%fused_computation.47 | convolution fusion | flops 110100192 | bytes 23186560 | tf_op jit(solution)/shard_map/co,oij->cij/dot_general | solution.py:77
  132.6 4.5 collective-permute-start.4
  138.5 98.4 %all-reduce = (f32[9,32]{1,0:T(8,128)S(1)}, f32[32,32]{1,0:T(8,128)S(1)}, f32[32,24]{0,1:T(8,128)S(1)}) all-reduce(f32[9,32]{1,0:T(8,128)S(1)} %stack.32, f32[32,32]{1,0:T(8,128)S(1)} %convolution_bitcast_fusion.2, f32[32,24]{0,1:T(8,128)S(1)} %fusion.30), channel_id=1, replica_groups=mesh['row'=16,'col'=32] {'row','col'}, use_global_device_ids=true, to_apply=%region_16.17 | all-reduce | flops 2080 | bytes 16640 | tf_op jit(solution)/shard_map/psum | solution.py:140
  242.3 3.6 copy.38
  246.0 3.6 copy.40
  251.5 3.6 collective-permute-start.6
  260.4 3.0 copy.41
  263.4 7.2 %pad_maximum_fusion.1 = (bf16[32,264,132]{2,0,1:T(8,128)(2,1)S(1)}, bf16[32,264,132]{2,0,1:T(8,128)(2,1)S(1)}) fusion(bf16[32,264,4]{2,0,1:T(8,128)(2,1)} %copy.39, bf16[32,4,128]{2,0,1:T(8,128)(2,1)S(1)} %collective-permute-done.5, bf16[32,256,128]{2,0,1:T(8,128)(2,1)} %copy-done.6, bf16[32,4,128]{2,0,1:T(8,128)(2,1)S(1)} %collective-permute-done.4, ...), kind=kLoop, calls=%fused_computation.22 | loop fusion | flops 17842176 | bytes 6758400 | tf_op jit(solution)/shard_map/concatenate | solution.py:24
  270.7 7.2 %fusion.48 = (f32[32,128]{1,0:T(8,128)S(1)}, f32[32,256]{0,1:T(8,128)S(1)}) fusion(bf16[32,264,132]{2,0,1:T(8,128)(2,1)S(1)} %get-tuple-element.30, f32[32]{0:T(128)S(1)} %get-tuple-element.48, bf16[32,256,128]{2,0,1:T(8,128)(2,1)S(1)} %copy-done.7, bf16[32,4,128]{2,0,1:T(8,128)(2,1)S(1)} %collective-permute-done.4, f32[32]{0:T(128)S(1)} %get-tuple-element.49, ...), kind=kLoop, calls=%fused_computation.101 | loop fusion | flops 33542144 | bytes 16893056 | tf_op jit(solution)/shard_map/reduce_sum | solution.py:116
  278.0 79.5 %psum.58 = bf16[128,32]{0,1:T(8,128)(2,1)S(1)} all-reduce(f32[128,32]{0,1:T(8,128)S(1)} %bitcast.80), channel_id=1, replica_groups=mesh['row'=16,'col'=32] {'row'}, use_global_device_ids=true, to_apply=%region_4.5 | all-reduce | flops 4096 | bytes 24576 | tf_op jit(solution)/shard_map/psum | solution.py:124
  358.2 8.6 %all-to-all-start = ((bf16[32,128,32]{1,2,0:T(8,128)(2,1)}), bf16[32,128,32]{1,2,0:T(8,128)(2,1)S(1)}, u32[]{:S(2)}, u32[]{:S(2)}) async-start(bf16[32,128,32]{1,2,0:T(8,128)(2,1)} %stack.22), calls=%async_computation | async-start | bytes 524288 | tf_op jit(solution)/shard_map/all_to_all | solution.py:126
  367.5 104.4 %psum.57 = bf16[256,32]{1,0:T(8,128)(2,1)S(1)} all-reduce(f32[256,32]{1,0:T(8,128)S(1)} %bitcast.79), channel_id=1, replica_groups=mesh['row'=16,'col'=32] {'col'}, use_global_device_ids=true, to_apply=%region_2.3 | all-reduce | flops 8192 | bytes 49152 | tf_op jit(solution)/shard_map/psum | solution.py:123
  474.8 162.8 %all-reduce.4.cloned.1.call-done = (f32[512,32]{0,1:T(8,128)}, f32[512,32]{0,1:T(8,128)}) async-done(((f32[512,32]{0,1:T(8,128)}, f32[512,32]{0,1:T(8,128)}), (f32[512,32]{0,1:T(8,128)}, f32[512,32]{0,1:T(8,128)})) %all-reduce.4.cloned.1.call-update) | async-done | bytes 131088 | tf_op jit(solution)/shard_map/psum | solution.py:141
  (70 shorter events, 37.8 us)
Async XLA Ops:
  7.2 57.6 %copy-start = (bf16[24,256,128]{2,1,0:T(8,128)(2,1)S(1)}, bf16[24,256,128]{2,1,0:T(8,128)(2,1)}, u32[]{:S(2)}) copy-start(bf16[24,256,128]{2,1,0:T(8,128)(2,1)} %param.13) | copy-start | bytes 4718596
  62.2 8.0 %copy-start.1 = (bf16[32,256,128]{2,0,1:T(8,128)(2,1)}, bf16[32,256,128]{2,0,1:T(8,128)(2,1)S(1)}, u32[]{:S(2)}) copy-start(bf16[32,256,128]{2,0,1:T(8,128)(2,1)S(1)} %add_convert_fusion) | copy-start | bytes 6291460
  62.2 6.1 collective-permute-start
  63.5 6.7 %collective-permute-start.1 = (bf16[32,4,128]{2,0,1:T(8,128)(2,1)S(1)}, bf16[32,4,128]{2,0,1:T(8,128)(2,1)S(1)}, u32[]{:S(2)}, u32[]{:S(2)}) collective-permute-start(bf16[32,4,128]{2,0,1:T(8,128)(2,1)S(1)} %get-tuple-element.40), channel_id=1, source_target_pairs={{32,0},{64,32},{96,64},{128,96},{160,128},{192,160},{224,192},{256... | collective-permute-start | bytes 98312 | tf_op jit(solution)/shard_map/ppermute | solution.py:23
  73.4 11.8 %copy-start.13 = (f32[9,32]{1,0:T(8,128)S(1)}, f32[9,32]{1,0:T(8,128)}, u32[]{:S(2)}) copy-start(f32[9,32]{1,0:T(8,128)} %param.10) | copy-start | bytes 3460
  80.7 10.9 %collective-permute-start.3 = (bf16[32,264,4]{1,0,2:T(8,128)(2,1)S(1)}, bf16[32,264,4]{1,0,2:T(8,128)(2,1)S(1)}, u32[]{:S(2)}, u32[]{:S(2)}) collective-permute-start(bf16[32,264,4]{1,0,2:T(8,128)(2,1)S(1)} %copy.36), channel_id=1, source_target_pairs={{1,0},{2,1},{3,2},{4,3},{5,4},{6,5},{7,6},{8,7},{9,8},{10,9},{11,1... | collective-permute-start | bytes 202760 | tf_op jit(solution)/shard_map/ppermute | solution.py:23
  82.6 5.9 collective-permute-start.2
  94.6 7.2 %copy-start.2 = (bf16[32,256,128]{2,0,1:T(8,128)(2,1)S(1)}, bf16[32,256,128]{2,0,1:T(8,128)(2,1)}, u32[]{:S(2)}) copy-start(bf16[32,256,128]{2,0,1:T(8,128)(2,1)} %copy-done.1) | copy-start | bytes 6291460
  101.9 10.2 %copy-start.4 = (bf16[32,264,132]{2,0,1:T(8,128)(2,1)}, bf16[32,264,132]{2,0,1:T(8,128)(2,1)S(1)}, u32[]{:S(2)}) copy-start(bf16[32,264,132]{2,0,1:T(8,128)(2,1)S(1)} %get-tuple-element.33) | copy-start | bytes 6690820
  101.9 10.2 %copy-start.5 = (bf16[32,264,132]{2,0,1:T(8,128)(2,1)}, bf16[32,264,132]{2,0,1:T(8,128)(2,1)S(1)}, u32[]{:S(2)}) copy-start(bf16[32,264,132]{2,0,1:T(8,128)(2,1)S(1)} %get-tuple-element.34) | copy-start | bytes 6690820
  101.9 10.2 %copy-start.14 = (bf16[32,32]{1,0:T(8,128)(2,1)S(1)}, bf16[32,32]{1,0:T(8,128)(2,1)}, u32[]{:S(2)}) copy-start(bf16[32,32]{1,0:T(8,128)(2,1)} %param.11) | copy-start | bytes 6148
  115.5 3.1 copy-start.3
  115.5 3.5 copy-start.8
  132.6 104.9 %collective-permute-start.4 = (bf16[32,4,128]{2,0,1:T(8,128)(2,1)S(1)}, bf16[32,4,128]{2,0,1:T(8,128)(2,1)S(1)}, u32[]{:S(2)}, u32[]{:S(2)}) collective-permute-start(bf16[32,4,128]{2,0,1:T(8,128)(2,1)S(1)} %get-tuple-element.37), channel_id=1, source_target_pairs={{0,32},{32,64},{64,96},{96,128},{128,160},{160,192},{192,224},{224... | collective-permute-start | bytes 98312 | tf_op jit(solution)/shard_map/ppermute | solution.py:22
  137.1 100.4 %collective-permute-start.5 = (bf16[32,4,128]{2,0,1:T(8,128)(2,1)S(1)}, bf16[32,4,128]{2,0,1:T(8,128)(2,1)S(1)}, u32[]{:S(2)}, u32[]{:S(2)}) collective-permute-start(bf16[32,4,128]{2,0,1:T(8,128)(2,1)S(1)} %get-tuple-element.38), channel_id=1, source_target_pairs={{32,0},{64,32},{96,64},{128,96},{160,128},{192,160},{224,192},{256... | collective-permute-start | bytes 98312 | tf_op jit(solution)/shard_map/ppermute | solution.py:23
  249.6 10.8 %collective-permute-start.7 = (bf16[32,264,4]{1,0,2:T(8,128)(2,1)S(1)}, bf16[32,264,4]{1,0,2:T(8,128)(2,1)S(1)}, u32[]{:S(2)}, u32[]{:S(2)}) collective-permute-start(bf16[32,264,4]{1,0,2:T(8,128)(2,1)S(1)} %copy.40), channel_id=1, source_target_pairs={{0,1},{1,2},{2,3},{3,4},{4,5},{5,6},{6,7},{7,8},{8,9},{9,10},{10,1... | collective-permute-start | bytes 202760 | tf_op jit(solution)/shard_map/ppermute | solution.py:22
  251.5 5.8 collective-permute-start.6
  263.4 7.2 %copy-start.7 = (bf16[32,256,128]{2,0,1:T(8,128)(2,1)S(1)}, bf16[32,256,128]{2,0,1:T(8,128)(2,1)}, u32[]{:S(2)}) copy-start(bf16[32,256,128]{2,0,1:T(8,128)(2,1)} %copy-done.6) | copy-start | bytes 6291460
  263.4 7.2 %copy-start.9 = (bf16[32,256,128]{2,0,1:T(8,128)(2,1)S(1)}, bf16[32,256,128]{2,0,1:T(8,128)(2,1)}, u32[]{:S(2)}) copy-start(bf16[32,256,128]{2,0,1:T(8,128)(2,1)} %multiply_convert_fusion.1) | copy-start | bytes 6291460
  270.7 201.2 %copy-start.10 = (bf16[256,512]{1,0:T(8,128)(2,1)S(1)}, bf16[256,512]{1,0:T(8,128)(2,1)}, u32[]{:S(2)}) copy-start(bf16[256,512]{1,0:T(8,128)(2,1)} %param.7) | copy-start | bytes 786436
  270.7 202.0 %copy-start.11 = (bf16[512,32]{0,1:T(8,128)(2,1)S(1)}, bf16[512,32]{0,1:T(8,128)(2,1)}, u32[]{:S(2)}) copy-start(bf16[512,32]{0,1:T(8,128)(2,1)} %param.8) | copy-start | bytes 98308
  270.7 203.1 %copy-start.12 = (bf16[512,32]{0,1:T(8,128)(2,1)S(1)}, bf16[512,32]{0,1:T(8,128)(2,1)}, u32[]{:S(2)}) copy-start(bf16[512,32]{0,1:T(8,128)(2,1)} %param.9) | copy-start | bytes 98308
  358.2 114.7 %all-to-all-start = ((bf16[32,128,32]{1,2,0:T(8,128)(2,1)}), bf16[32,128,32]{1,2,0:T(8,128)(2,1)S(1)}, u32[]{:S(2)}, u32[]{:S(2)}) async-start(bf16[32,128,32]{1,2,0:T(8,128)(2,1)} %stack.22), calls=%async_computation | async-start | bytes 524288 | tf_op jit(solution)/shard_map/all_to_all | solution.py:126
  366.9 270.7 %all-reduce.4.cloned.1.call-start = ((), (), s32[]{:S(2)}) async-start(), calls=%async_computation.1 | async-start | bytes 262144 | tf_op jit(solution)/shard_map/psum | solution.py:141
  (1 other events, 1.3 us)
Sparse Core Ops, SparseCore 0:
  473.9 163.6 all-reduce.3
